TPU v7x, 32 devices: a whole 2x2x4 slice. The times are simulated.
32 devices in a mesh: vec: 8 (over z, y), space: 4 (over x, core).
Axes of the slice: x: 2, y: 2, z: 4, core: 2. Of those that a mesh axis runs over, the one named last changes fastest.
Arguments:
- perturbation: float32 [8, 6, 96, 512], P('vec', None, 'space'), may hold values from -40 to 40
- trajectory: bfloat16 [8, 3, 6, 96, 512], P('vec', None, None, 'space'), may hold values from -1.796875 to 1.796875
- step_order: int32 [8], replicated, may hold values from 0 to 7, each once
Outputs:
- ortho_vectors: float32 [8, 6, 96, 512], P('vec', None, 'space')
- upper_factor: float32 [8, 8], replicated
Inputs may be any that keep to these rules, and one draw needn't show every extreme that they name: `step_order`: each number appears once.
All inputs are finite; a program needn't handle non-finite values.
Results may differ from a plain program's by a relative error of at most 0.0003.
Values may be sent and summed in bfloat16 or wider, within the bound.
A program may use at most 64 MiB of HBM per device.

v0:
```python
import functools

import jax
import jax.numpy as jnp
from jax import lax
from jax.experimental import pallas as pl
from jax.experimental.pallas import tpu as pltpu
from jax.sharding import PartitionSpec as P

STEPS = 2
SECTIONS = 3
RIM_LAG = 10
LAG = 6
HALO = 8

GRAVITY_TOP = 1.0
GRAVITY_LOW = 0.5
DEPTH_TOP = 1.0
DEPTH_LOW = 1.0
CORIOLIS = 0.3
TIME_STEP = 0.25

MESH = pl.DeviceIdType.MESH
F32 = jnp.float32


def remote(src, dst, send, recv, target):
    return pltpu.make_async_remote_copy(
        src_ref=src, dst_ref=dst, send_sem=send, recv_sem=recv, device_id=target, device_id_type=MESH
    )


def diff_x(field):
    count = field.shape[0]
    return 0.5 * (pltpu.roll(field, count - 1, 0) - pltpu.roll(field, 1, 0))


def diff_y(field):
    count = field.shape[1]
    return 0.5 * (pltpu.roll(field, count - 1, 1) - pltpu.roll(field, 1, 1))


def tangent(base, state):
    dp_top = GRAVITY_TOP * (state[0] + state[3])
    dp_low = dp_top + GRAVITY_LOW * state[3]
    rates = []
    for layer, (mean_depth, pressure) in enumerate(((DEPTH_TOP, dp_top), (DEPTH_LOW, dp_low))):
        at = 3 * layer
        depth = base[at] + mean_depth
        u, v = base[at + 1], base[at + 2]
        dh, du, dv = state[at], state[at + 1], state[at + 2]
        rates.append(-diff_x(depth * du + dh * u) - diff_y(depth * dv + dh * v))
        rates.append(
            -(u * diff_x(du) + du * diff_x(u)) - (v * diff_y(du) + dv * diff_y(u))
            + CORIOLIS * dv - diff_x(pressure)
        )
        rates.append(
            -(u * diff_x(dv) + du * diff_x(v)) - (v * diff_y(dv) + dv * diff_y(v))
            - CORIOLIS * du - diff_y(pressure)
        )
    return rates


def tiles_of(fields, rows, cols):
    return [
        (f, r, l) for f in range(fields) for r in range(0, rows, 8) for l in range(0, cols, 128)
    ]


def whole_kernel(
    n, ns, direct, per, entries, order_ref, traj_ref, pert_ref,
    back, upper_ref,
    main, lo, hi, plo, phi, pair, in_up, in_dn, out_up, out_dn, edges, anchor, work,
    x_ref, cols_ref, result, gspace, gvec, mine_s, mine_v,
    sa, ra, su, ru, sd, rd, sc, rc, sh, rh, sp, rp,
    s1, r1, s2, r2, s3, r3, s4, r4,
):
    me = lax.axis_index("vec")
    tile = lax.axis_index("space")
    side = lax.rem(me, 2)
    line = me // 2
    lines = n // 2
    partner = me + 1 - 2 * side
    up_ok = line < lines - 1
    dn_ok = line > 0
    next_tile = lax.rem(tile + 1, ns)
    prev_tile = lax.rem(tile + ns - 1, ns)
    fields, rows, cols = pert_ref.shape
    chunks = STEPS * SECTIONS * 3
    parts = SECTIONS * 3

    barrier = pltpu.get_barrier_semaphore()
    pl.semaphore_signal(barrier, inc=1, device_id={"vec": partner}, device_id_type=MESH)
    near_tiles = (1, ns - 1) if ns <= 4 else range(1, ns)
    for d in near_tiles:
        pl.semaphore_signal(barrier, inc=1, device_id={"space": lax.rem(tile + d, ns)}, device_id_type=MESH)

    @pl.when(up_ok)
    def _():
        pl.semaphore_signal(barrier, inc=1, device_id={"vec": me + 2}, device_id_type=MESH)

    @pl.when(dn_ok)
    def _():
        pl.semaphore_signal(barrier, inc=1, device_id={"vec": me - 2}, device_id_type=MESH)

    pl.semaphore_wait(barrier, 1 + len(near_tiles) + up_ok.astype(jnp.int32) + dn_ok.astype(jnp.int32))

    def swap(p):
        k, f = lax.div(p, 3), lax.rem(p, 3)
        return remote(
            traj_ref.at[k, 3 * (1 - side) + f], pair.at[p], sa.at[p], ra.at[p], {"vec": partner}
        )

    def go_up(c):
        return remote(out_up.at[c], in_up.at[c], su.at[c], ru.at[c], {"vec": me + 2})

    def go_dn(c):
        return remote(out_dn.at[c], in_dn.at[c], sd.at[c], rd.at[c], {"vec": me - 2})

    def give(c):
        place = main.at[lax.div(c, 3), 3 * side + lax.rem(c, 3)]
        return remote(place, place, sc.at[c], rc.at[c], {"vec": partner})

    def edge_next(c):
        return remote(edges.at[c, 1], lo.at[c], sh.at[c, 1], rh.at[c, 1], {"space": next_tile})

    def edge_prev(c):
        return remote(edges.at[c, 0], hi.at[c], sh.at[c, 0], rh.at[c, 0], {"space": prev_tile})

    pert_next = remote(pert_ref.at[:, pl.ds(rows - HALO, HALO)], plo, sp.at[0], rp.at[0], {"space": next_tile})
    pert_prev = remote(pert_ref.at[:, pl.ds(0, HALO)], phi, sp.at[1], rp.at[1], {"space": prev_tile})

    @pl.loop(0, parts)
    def _(p):
        swap(p).start()

    pert_next.start()
    pert_prev.start()

    def owner_of(c):
        return jnp.where(c >= parts, order_ref[1], order_ref[0])

    def candidate(c):
        p = lax.rem(c, parts)
        own = traj_ref[lax.div(p, 3), 3 * side + lax.rem(p, 3)]
        return jnp.where(owner_of(c) == me, own, pair[p])

    def inside(c):
        return (c >= 0) & (c < chunks)

    near = LAG * jnp.minimum(line, lines - 1 - line)
    far = LAG * jnp.maximum(line, lines - 1 - line)
    anchor[:, HALO : HALO + rows] = pert_ref[...]

    @pl.loop(0, LAG * (lines - 1) + chunks + LAG + RIM_LAG)
    def _(t):
        c_pair = t - near
        c_up = t - LAG * line
        c_dn = t - LAG * (lines - 1 - line)
        c_fin = t - far
        c_edge = c_fin - LAG
        c_run = c_edge - RIM_LAG

        @pl.when((c_pair >= 0) & (c_pair < parts))
        def _():
            swap(c_pair).wait_recv()

        @pl.when(inside(c_up))
        def _():
            @pl.when(dn_ok)
            def _():
                go_up(c_up).wait_recv()

            @pl.when(up_ok)
            def _():
                here = lax.div(owner_of(c_up), 2) == line
                out_up[c_up] = jnp.where(here, candidate(c_up), in_up[c_up])
                go_up(c_up).start()

        @pl.when(inside(c_dn))
        def _():
            @pl.when(up_ok)
            def _():
                go_dn(c_dn).wait_recv()

            @pl.when(dn_ok)
            def _():
                here = lax.div(owner_of(c_dn), 2) == line
                out_dn[c_dn] = jnp.where(here, candidate(c_dn), in_dn[c_dn])
                go_dn(c_dn).start()

        @pl.when(inside(c_fin))
        def _():
            at = lax.div(owner_of(c_fin), 2)
            main[lax.div(c_fin, 3), 3 * side + lax.rem(c_fin, 3)] = jnp.where(
                at == line, candidate(c_fin), jnp.where(at < line, in_up[c_fin], in_dn[c_fin])
            )
            give(c_fin).start()

        @pl.when(inside(c_edge))
        def _():
            give(c_edge).wait_recv()

        @pl.when(inside(c_edge) & (lax.rem(c_edge, 3) == 2))
        def _():
            section = lax.div(c_edge, 3)
            edges[section, 0] = main[section, :, :HALO, :]
            edges[section, 1] = main[section, :, rows - HALO :, :]
            edge_next(section).start()
            edge_prev(section).start()

        @pl.when(c_run == 0)
        def _():
            pert_next.wait()
            pert_prev.wait()
            anchor[:, :HALO] = plo[...]
            anchor[:, HALO + rows :] = phi[...]
            work[...] = anchor[...]

        @pl.when(inside(c_run) & (lax.rem(c_run, 3) == 2))
        def _():
            number = lax.div(c_run, 3)
            section = lax.rem(number, SECTIONS)
            edge_next(number).wait()
            edge_prev(number).wait()
            base = [
                jnp.concatenate(
                    [
                        lo[number, f].astype(F32),
                        main[number, f].astype(F32),
                        hi[number, f].astype(F32),
                    ],
                    axis=0,
                )
                for f in range(fields)
            ]
            current = [work[f] for f in range(fields)]
            change = tangent(base, current)
            keep = jnp.where(section == 0, 0.0, jnp.where(section == 1, 0.75, 1.0 / 3.0)).astype(F32)
            take = jnp.where(section == 0, 1.0, jnp.where(section == 1, 0.25, 2.0 / 3.0)).astype(F32)
            for f in range(fields):
                work[f] = keep * anchor[f] + take * (current[f] + TIME_STEP * change[f])

            @pl.when(section == SECTIONS - 1)
            def _():
                anchor[...] = work[...]

    units = tiles_of(fields, rows, cols)
    for number, (f, r, l) in enumerate(units):
        x_ref[number // per, pl.ds((number % per) * 8, 8), :] = work[
            f, HALO + r : HALO + r + 8, l : l + 128
        ]
    for number in range(len(units), n * per):
        x_ref[number // per, pl.ds((number % per) * 8, 8), :] = jnp.zeros((8, 128), F32)

    def peers(count, here, axis, src, dst, send, recv):
        made = []
        for d in range(1, count):
            to = lax.rem(here + d, count)
            made.append(remote(src(to), dst, send.at[d], recv.at[d], {axis: to}))
        return made

    first = peers(n, me, "vec", lambda to: x_ref.at[to], cols_ref.at[me], s1, r1)
    for copy in first:
        copy.start()
    cols_ref[me] = x_ref[me]

    @pl.loop(0, parts)
    def _(p):
        swap(p).wait_send()

    @pl.loop(0, chunks)
    def _(c):
        give(c).wait_send()

        @pl.when(up_ok)
        def _():
            go_up(c).wait_send()

        @pl.when(dn_ok)
        def _():
            go_dn(c).wait_send()

    for copy in first:
        copy.wait_recv()

    lanes = lax.broadcasted_iota(jnp.int32, (n, 128), 1)
    rows = lax.broadcasted_iota(jnp.int32, (n, 128), 0)
    gram = jnp.zeros((n, 128), F32)
    for i in range(n):
        line = jnp.sum(cols_ref[...] * cols_ref[i][None], axis=1)
        gram = gram + jnp.where(lanes == i, jnp.sum(line, axis=1, keepdims=True), 0.0)

    everyone = []
    if direct:
        mine_s[...] = gram
        for e in range(1, n * ns):
            dv, ds = e // ns, e % ns
            place = gvec.at[me * ns + tile]
            where = {"vec": lax.rem(me + dv, n), "space": lax.rem(tile + ds, ns)}
            everyone.append(remote(mine_s, place, s3.at[e], r3.at[e], where))
        everyone.reverse()
        for copy in everyone:
            copy.start()
        gvec[me * ns + tile] = gram
        for copy in everyone:
            copy.wait_recv()
        gram = gvec[0]
        for i in range(1, n * ns):
            gram = gram + gvec[i]
    else:
        mine_s[...] = gram
        second = peers(ns, tile, "space", lambda to: mine_s, gspace.at[tile], s2, r2)
        everyone += second
        for copy in second:
            copy.start()
        gspace[tile] = gram
        for copy in second:
            copy.wait_recv()
        gram = gspace[0]
        for i in range(1, ns):
            gram = gram + gspace[i]

        mine_v[...] = gram
        third = peers(n, me, "vec", lambda to: mine_v, gvec.at[me], s3, r3)
        everyone += third
        for copy in third:
            copy.start()
        gvec[me] = gram
        for copy in third:
            copy.wait_recv()
        gram = gvec[0]
        for i in range(1, n):
            gram = gram + gvec[i]

    a = jnp.where(lanes < n, gram / entries, 0.0) + jnp.where(lanes == rows + n, 1.0, 0.0)
    for k in range(n):
        pivot_row = a[k : k + 1, :]
        column = jnp.sum(jnp.where(lanes == k, a, 0.0), axis=1, keepdims=True)
        factor = jnp.where(rows[:, :1] > k, column / column[k : k + 1, :], 0.0)
        a = a - factor * pivot_row
    diagonal = jnp.sum(jnp.where(lanes == rows, a, 0.0), axis=1, keepdims=True)
    a = a / jnp.sqrt(diagonal)
    upper_ref[...] = jnp.where(lanes >= rows, a, 0.0)

    for i in range(n):
        total = jnp.broadcast_to(a[i : i + 1, n : n + 1], cols_ref.shape[1:]) * cols_ref[0]
        for j in range(1, i + 1):
            total = total + jnp.broadcast_to(a[i : i + 1, n + j : n + j + 1], cols_ref.shape[1:]) * cols_ref[j]
        result[i] = total

    fourth = peers(n, me, "vec", lambda to: result.at[to], back.at[me], s4, r4)
    for copy in fourth:
        copy.start()
    back[me] = result[me]
    for copy in fourth:
        copy.wait_recv()
    for copy in first + everyone + fourth:
        copy.wait_send()


def body(n, ns, perturbation, trajectory, step_order):
    pert, traj = perturbation[0], trajectory[0]
    fields, rows, cols = pert.shape
    count = fields * (rows // 8) * (cols // 128)
    per = -(-count // n)
    sections = traj.shape[0]
    direct = n * ns <= 64
    slots = n * ns if direct else n
    chunks, bf = STEPS * sections * 3, traj.dtype
    vmem = pl.BlockSpec(memory_space=pltpu.VMEM)
    piece = pltpu.VMEM((chunks, rows, cols), bf)
    rim = pltpu.VMEM((STEPS * sections, fields, HALO, cols), bf)
    fringe = pltpu.VMEM((fields, HALO, cols), F32)
    full = pltpu.VMEM((fields, rows + 2 * HALO, cols), F32)
    slices = pltpu.VMEM((n, per * 8, 128), F32)
    small = pltpu.VMEM((n, 128), F32)
    dma = pltpu.SemaphoreType.DMA
    back, upper = pl.pallas_call(
        functools.partial(whole_kernel, n, ns, direct, per, float(fields * rows * cols * ns)),
        out_shape=(
            jax.ShapeDtypeStruct((n, per * 8, 128), F32),
            jax.ShapeDtypeStruct((n, 128), F32),
        ),
        in_specs=[pl.BlockSpec(memory_space=pltpu.SMEM), vmem, vmem],
        out_specs=(vmem, vmem),
        scratch_shapes=[
            pltpu.VMEM((STEPS * sections, fields, rows, cols), bf),
            rim, rim, fringe, fringe,
            pltpu.VMEM((sections * 3, rows, cols), bf),
            piece, piece, piece, piece,
            pltpu.VMEM((STEPS * sections, 2, fields, HALO, cols), bf),
            full, full,
            slices, slices, slices,
            pltpu.VMEM((ns, n, 128), F32), pltpu.VMEM((slots, n, 128), F32), small, small,
            dma((sections * 3,)), dma((sections * 3,)),
            dma((chunks,)), dma((chunks,)),
            dma((chunks,)), dma((chunks,)),
            dma((chunks,)), dma((chunks,)),
            dma((STEPS * sections, 2)), dma((STEPS * sections, 2)),
            dma((2,)), dma((2,)),
            dma((n,)), dma((n,)), dma((ns,)), dma((ns,)),
            dma((slots,)), dma((slots,)), dma((n,)), dma((n,)),
        ],
        compiler_params=pltpu.CompilerParams(collective_id=0, has_side_effects=True),
        name="whole",
    )(step_order, traj, pert)
    def finish(back_ref, upper_ref, out_ref, factor_ref):
        for number, (f, r, l) in enumerate(tiles_of(fields, rows, cols)):
            out_ref[f, r : r + 8, l : l + 128] = back_ref[number // per, pl.ds((number % per) * 8, 8), :]
        factor_ref[...] = upper_ref[:, :n]

    out, factor = pl.pallas_call(
        finish,
        out_shape=(jax.ShapeDtypeStruct(pert.shape, F32), jax.ShapeDtypeStruct((n, n), F32)),
        in_specs=[vmem, vmem],
        out_specs=(vmem, vmem),
        name="finish",
    )(back, upper)
    return out[None], factor


def solution(mesh):
    n, ns = mesh.shape["vec"], mesh.shape["space"]
    in_specs = (P("vec", None, "space", None), P("vec", None, None, "space", None), P())
    out_specs = (P("vec", None, "space", None), P())
    return jax.shard_map(
        functools.partial(body, n, ns), mesh=mesh, in_specs=in_specs, out_specs=out_specs, check_vma=False
    )
```

profile of v0, /device:TPU:0, one launch (start us, length us, event | category | flops | bytes accessed | tf_op | source)
XLA Modules:
  0.0 58.2 jit_solution(10255544465138290818)
XLA Ops:
  0.6 55.9 %whole.1 = (f32[8,72,128]{2,1,0:T(8,128)}, f32[8,128]{1,0:T(8,128)}) custom-call(s32[8]{0:T(128)} %order_ref.1, bf16[3,6,24,512]{3,2,1,0:T(8,128)(2,1)} %bitcast.3, f32[6,24,512]{2,1,0:T(8,128)} %bitcast.4), custom_call_target="tpu_custom_call" | custom-call | tf_op jit(solution)/shard_map/whole/pallas_call | solution.py:379
  56.5 1.7 %finish.1 = (f32[6,24,512]{2,1,0:T(8,128)}, f32[8,8]{1,0:T(8,128)}) custom-call(f32[8,72,128]{2,1,0:T(8,128)} %get-tuple-element.6.back_ref, f32[8,128]{1,0:T(8,128)} %get-tuple-element.7.upper_ref), custom_call_target="tpu_custom_call" | custom-call | tf_op jit(solution)/shard_map/finish/pallas_call | solution.py:413
where the time goes:
time: 58.4 us; the launch traced here: 58.2 us
  Pallas kernels  57.6 us (99%)
  between operations  0.64 us (1%)
    pallas_call x1, Pallas kernels, body(): pl.pallas_call(functools.partial(whole_kernel, n, ns, direct, per, float(...  55.9 us
    pallas_call x1, Pallas kernels, body(): pl.pallas_call(finish, out_shape=(jax.ShapeDtypeStruct(pert.shape, F32),...  1.7 us

commit v1 on v0

v1 whole, which is shorter than its diff:
```python
import functools

import jax
import jax.numpy as jnp
from jax import lax
from jax.experimental import pallas as pl
from jax.experimental.pallas import tpu as pltpu
from jax.sharding import PartitionSpec as P

STEPS = 2
SECTIONS = 3
LAG = 4
RUN_LAG = 3
HALO = 8

GRAVITY_TOP = 1.0
GRAVITY_LOW = 0.5
DEPTH_TOP = 1.0
DEPTH_LOW = 1.0
CORIOLIS = 0.3
TIME_STEP = 0.25

MESH = pl.DeviceIdType.MESH
F32 = jnp.float32


def remote(src, dst, send, recv, target):
    return pltpu.make_async_remote_copy(
        src_ref=src, dst_ref=dst, send_sem=send, recv_sem=recv, device_id=target, device_id_type=MESH
    )


def await_bytes(ref, sem):
    pltpu.make_async_copy(ref, ref, sem).wait()


def diff_x(field):
    count = field.shape[0]
    return 0.5 * (pltpu.roll(field, count - 1, 0) - pltpu.roll(field, 1, 0))


def diff_y(field):
    count = field.shape[1]
    return 0.5 * (pltpu.roll(field, count - 1, 1) - pltpu.roll(field, 1, 1))


def tangent(base, state):
    dp_top = GRAVITY_TOP * (state[0] + state[3])
    dp_low = dp_top + GRAVITY_LOW * state[3]
    rates = []
    for layer, (mean_depth, pressure) in enumerate(((DEPTH_TOP, dp_top), (DEPTH_LOW, dp_low))):
        at = 3 * layer
        depth = base[at] + mean_depth
        u, v = base[at + 1], base[at + 2]
        dh, du, dv = state[at], state[at + 1], state[at + 2]
        rates.append(-diff_x(depth * du + dh * u) - diff_y(depth * dv + dh * v))
        rates.append(
            -(u * diff_x(du) + du * diff_x(u)) - (v * diff_y(du) + dv * diff_y(u))
            + CORIOLIS * dv - diff_x(pressure)
        )
        rates.append(
            -(u * diff_x(dv) + du * diff_x(v)) - (v * diff_y(dv) + dv * diff_y(v))
            - CORIOLIS * du - diff_y(pressure)
        )
    return rates


def slice_shape(n, fields, cols):
    lanes = cols // 128
    best = None
    for f in range(1, fields + 1):
        for l in range(1, lanes + 1):
            if fields % f or lanes % l or (fields // f) * (lanes // l) > n:
                continue
            if best is None or f * l < best[0] * best[1]:
                best = (f, l)
    return best


def whole_kernel(
    n, ns, entries, order_ref, traj_ref, pert_ref,
    out_ref, upper_ref,
    main, cand, in_up, in_dn, out_up, out_dn, pool, fresh, rims, anchor, work,
    x_ref, cols_ref, result, gspace, gvec, mine_s, mine_v,
    r_cand, r_up, r_dn, r_sec, r_pert, r_vec, r_gs, r_gv, r_back,
    s_cand, s_pert, s_up, s_dn, s_give, s_edge, s_vec, s_gs, s_gv, s_back,
):
    me = lax.axis_index("vec")
    tile = lax.axis_index("space")
    fields, rows, cols = pert_ref.shape
    half = fields // 2
    chunks = STEPS * SECTIONS * half
    parts = SECTIONS * half
    lines, places = n // 2, ns // 2
    side, line = lax.rem(me, 2), me // 2
    core, place = lax.rem(tile, 2), tile // 2
    flip = lax.rem(place, 2)

    def differs(a, b):
        return a + b - 2 * a * b

    home = differs(side, flip)
    stay = core == home
    away = core != home
    block = 2 * place + home
    vector = 2 * line + differs(core, flip)
    sibling = {"space": 2 * place + 1 - core}
    up_ok = line < lines - 1
    dn_ok = line > 0

    def worker(v, t):
        p = t // 2
        turn = lax.rem(p, 2)
        return {
            "vec": 2 * (v // 2) + differs(lax.rem(t, 2), turn),
            "space": 2 * p + differs(lax.rem(v, 2), turn),
        }

    barrier = pltpu.get_barrier_semaphore()
    near = sorted({0, 1 % places, places - 1})
    count = 0
    for across in range(2):
        for step in near:
            for c in range(2):
                if across == 0 and step == 0 and c == 0:
                    continue
                where = {
                    "vec": me + across * (1 - 2 * side),
                    "space": 2 * lax.rem(place + step, places) + lax.rem(core + c, 2),
                }
                pl.semaphore_signal(barrier, inc=1, device_id=where, device_id_type=MESH)
                count += 1

    @pl.when(up_ok)
    def _():
        pl.semaphore_signal(barrier, inc=1, device_id={"vec": me + 2}, device_id_type=MESH)

    @pl.when(dn_ok)
    def _():
        pl.semaphore_signal(barrier, inc=1, device_id={"vec": me - 2}, device_id_type=MESH)

    inner = pl.ds(HALO, rows)

    @pl.when(stay)
    def _():
        @pl.loop(0, parts)
        def _(p):
            k, f = lax.div(p, half), lax.rem(p, half)
            pltpu.make_async_copy(traj_ref.at[k, half * core + f], cand.at[0, p], r_cand.at[p]).start()

        pltpu.make_async_copy(pert_ref, anchor.at[:, inner], r_pert).start()

    pl.semaphore_wait(barrier, count + up_ok.astype(jnp.int32) + dn_ok.astype(jnp.int32))

    other = me + 1 - 2 * side

    @pl.when(stay)
    def _():
        @pl.loop(0, parts)
        def _(p):
            k, f = lax.div(p, half), lax.rem(p, half)
            remote(
                traj_ref.at[k, half * (1 - core) + f], cand.at[0, p], s_cand, r_cand.at[p], sibling
            ).start()

    @pl.when(away)
    def _():
        @pl.loop(0, parts)
        def _(p):
            k, f = lax.div(p, half), lax.rem(p, half)
            for c in range(2):
                remote(
                    traj_ref.at[k, half * c + f], cand.at[1, p], s_cand, r_cand.at[p],
                    {"vec": other, "space": 2 * place + c},
                ).start()

    next_tile = lax.rem(tile + 1, ns)
    prev_tile = lax.rem(tile + ns - 1, ns)
    remote(
        pert_ref.at[:, pl.ds(rows - HALO, HALO)], anchor.at[:, pl.ds(0, HALO)], s_pert, r_pert,
        worker(me, next_tile),
    ).start()
    remote(
        pert_ref.at[:, pl.ds(0, HALO)], anchor.at[:, pl.ds(HALO + rows, HALO)], s_pert, r_pert,
        worker(me, prev_tile),
    ).start()

    @pl.when(away)
    def _():
        remote(
            pert_ref, anchor.at[:, inner], s_pert, r_pert,
            {"vec": other, "space": 2 * place + 1 - core},
        ).start()

    def go_up(c):
        return remote(out_up.at[c], in_up.at[c], s_up, r_up.at[c], {"vec": me + 2})

    def go_dn(c):
        return remote(out_dn.at[c], in_dn.at[c], s_dn, r_dn.at[c], {"vec": me - 2})

    def owner_of(c):
        return jnp.where(c >= parts, order_ref[1], order_ref[0])

    def candidate(c):
        p = lax.rem(c, parts)
        return jnp.where(owner_of(c) == me, cand[0, p], cand[1, p])

    def inside(c):
        return (c >= 0) & (c < chunks)

    first_block = worker(vector, lax.rem(block + 1, ns))
    last_block = worker(vector, lax.rem(block + ns - 1, ns))
    own_layer = pl.ds(half * core, half)

    near_lag = LAG * jnp.minimum(line, lines - 1 - line)
    far_lag = LAG * jnp.maximum(line, lines - 1 - line)

    def advance(number, section, last):
        base = [main[number, f].astype(F32) for f in range(fields)]
        current = [work[f] for f in range(fields)]
        change = tangent(base, current)
        if last:
            keep, take = 1.0 / 3.0, 2.0 / 3.0
            mid = slice(HALO, HALO + rows)
            for f in range(fields):
                x_ref[f] = keep * anchor[f, mid] + take * (current[f][mid] + TIME_STEP * change[f][mid])
            return
        keep = jnp.where(section == 0, 0.0, jnp.where(section == 1, 0.75, 1.0 / 3.0)).astype(F32)
        take = jnp.where(section == 0, 1.0, jnp.where(section == 1, 0.25, 2.0 / 3.0)).astype(F32)
        for f in range(fields):
            work[f] = keep * anchor[f] + take * (current[f] + TIME_STEP * change[f])

        @pl.when(section == SECTIONS - 1)
        def _():
            anchor[...] = work[...]

    @pl.loop(0, LAG * (lines - 1) + chunks + RUN_LAG)
    def _(t):
        c_pair = t - near_lag
        c_up = t - LAG * line
        c_dn = t - LAG * (lines - 1 - line)
        c_fin = t - far_lag
        c_run = c_fin - RUN_LAG

        @pl.when((c_pair >= 0) & (c_pair < parts))
        def _():
            await_bytes(cand.at[:, c_pair], r_cand.at[c_pair])

        @pl.when(inside(c_up))
        def _():
            @pl.when(dn_ok)
            def _():
                go_up(c_up).wait_recv()

            @pl.when(up_ok)
            def _():
                here = lax.div(owner_of(c_up), 2) == line
                out_up[c_up] = jnp.where(here, candidate(c_up), in_up[c_up])
                go_up(c_up).start()

        @pl.when(inside(c_dn))
        def _():
            @pl.when(up_ok)
            def _():
                go_dn(c_dn).wait_recv()

            @pl.when(dn_ok)
            def _():
                here = lax.div(owner_of(c_dn), 2) == line
                out_dn[c_dn] = jnp.where(here, candidate(c_dn), in_dn[c_dn])
                go_dn(c_dn).start()

        @pl.when(inside(c_fin))
        def _():
            at = lax.div(owner_of(c_fin), 2)
            q, f = lax.div(c_fin, half), half * core + lax.rem(c_fin, half)
            main[q, f, inner] = jnp.where(
                at == line, candidate(c_fin), jnp.where(at < line, in_up[c_fin], in_dn[c_fin])
            )
            spot = main.at[q, f, inner]
            remote(spot, spot, s_give, r_sec.at[q], sibling).start()

            @pl.when(lax.rem(c_fin, half) == half - 1)
            def _():
                for c in range(2):
                    for target, src, dst in (
                        (first_block, rows, 0), (last_block, HALO, HALO + rows)
                    ):
                        remote(
                            main.at[q, own_layer, pl.ds(src, HALO)],
                            main.at[q, own_layer, pl.ds(dst, HALO)],
                            s_edge, r_sec.at[q],
                            {"vec": target["vec"], "space": 2 * (target["space"] // 2) + c},
                        ).start()

        @pl.when(c_run == half - 1)
        def _():
            await_bytes(anchor, r_pert)
            work[...] = anchor[...]

        @pl.when(inside(c_run) & (lax.rem(c_run, half) == half - 1))
        def _():
            number = lax.div(c_run, half)
            section = lax.rem(number, SECTIONS)
            await_bytes(fresh, r_sec.at[number])

            @pl.when(c_run < chunks - 1)
            def _():
                advance(number, section, False)

            @pl.when(c_run == chunks - 1)
            def _():
                advance(number, section, True)

    size_f, size_l = slice_shape(n, fields, cols)
    across = cols // (128 * size_l)
    slots = (fields // size_f) * across
    mine = 2 * line + core
    packed = n * n <= 128 and n % 8 == 0 and n * ns <= 64

    def slot(v):
        return n - 1 - v if packed else v

    def window(ref, j):
        f = pl.multiple_of(lax.div(j, across) * size_f, size_f)
        l = pl.multiple_of(lax.rem(j, across) * (128 * size_l), 128 * size_l)
        return ref.at[pl.ds(f, size_f), :, pl.ds(l, 128 * size_l)]

    def spread(d):
        to = lax.rem(mine + d, n)
        return to, {"vec": 2 * (to // 2) + side, "space": 2 * place + lax.rem(to, 2)}

    order = [d for d in sorted(range(1, n), key=lambda d: -min(d, n - d))]
    for d in order:
        to, where = spread(d)

        @pl.when(to < slots)
        def _():
            remote(window(x_ref, to), cols_ref.at[slot(vector)], s_vec, r_vec, where).start()

    @pl.when(mine < slots)
    def _():
        cols_ref[slot(vector)] = window(x_ref, mine)[...]

    @pl.when(stay)
    def _():
        await_bytes(pool.at[pl.ds(0, parts)], s_cand)
        await_bytes(anchor.at[:, pl.ds(0, 2 * HALO)], s_pert)

    @pl.when(away)
    def _():
        await_bytes(pool.at[pl.ds(0, 2 * parts)], s_cand)
        await_bytes(anchor, s_pert)

    await_bytes(out_up, s_give)
    await_bytes(rims, s_edge)

    @pl.when(up_ok)
    def _():
        await_bytes(out_up, s_up)

    @pl.when(dn_ok)
    def _():
        await_bytes(out_dn, s_dn)

    lanes = lax.broadcasted_iota(jnp.int32, (n, 128), 1)
    ranks = lax.broadcasted_iota(jnp.int32, (n, 128), 0)

    @pl.when(mine < slots)
    def _():
        await_bytes(cols_ref.at[pl.ds(0, n - 1)], r_vec)
        gram = jnp.zeros((n, 128), F32)
        for i in range(n):
            total = jnp.sum(cols_ref[...] * cols_ref[slot(i)][None], axis=(1, 2))
            if total.shape[-1] != 128:
                total = total.reshape(n, size_l, 128).sum(axis=1)
            gram = gram + jnp.where(lanes == i, jnp.sum(total, axis=1, keepdims=True), 0.0)
        mine_s[...] = gram

    @pl.when(mine >= slots)
    def _():
        mine_s[...] = jnp.zeros((n, 128), F32)

    if packed:
        row = jnp.sum(pltpu.roll(mine_s[...], 0, 1, stride=n, stride_axis=0), axis=0, keepdims=True)
        mine_v[...] = row
        rank = me * ns + tile
        reach = [(dv, ds) for dv in range(n) for ds in range(ns) if dv or ds]
        reach.sort(key=lambda e: -min(e[0], n - e[0]))
        for dv, ds in reach:
            where = {"vec": lax.rem(me + dv, n), "space": lax.rem(tile + ds, ns)}
            remote(mine_v, gvec.at[rank], s_gv, r_gv, where).start()
        gvec[rank] = row
        await_bytes(gvec.at[pl.ds(0, n * ns - 1)], r_gv)
        row = gvec[0]
        for i in range(1, n * ns):
            row = row + gvec[i]
        gram = pltpu.roll(jnp.broadcast_to(row, (n, 128)), 128 - n * (n - 1), 1, stride=n, stride_axis=0)
    else:
        for d in range(1, ns):
            to = lax.rem(tile + d, ns)
            remote(mine_s, gspace.at[tile], s_gs, r_gs, {"space": to}).start()
        gspace[tile] = mine_s[...]
        await_bytes(gspace.at[pl.ds(0, ns - 1)], r_gs)
        gram = gspace[0]
        for i in range(1, ns):
            gram = gram + gspace[i]
        mine_v[...] = gram
        for d in range(1, n):
            to = lax.rem(me + d, n)
            remote(mine_v, gvec.at[me], s_gv, r_gv, {"vec": to}).start()
        gvec[me] = gram
        await_bytes(gvec.at[pl.ds(0, n - 1)], r_gv)
        gram = gvec[0]
        for i in range(1, n):
            gram = gram + gvec[i]

    a = jnp.where(lanes < n, gram / entries, 0.0) + jnp.where(lanes == ranks + n, 1.0, 0.0)
    for k in range(n):
        pivot_row = a[k : k + 1, :]
        column = jnp.sum(jnp.where(lanes == k, a, 0.0), axis=1, keepdims=True)
        factor = jnp.where(ranks[:, :1] > k, column / column[k : k + 1, :], 0.0)
        a = a - factor * pivot_row
    diagonal = jnp.sum(jnp.where(lanes == ranks, a, 0.0), axis=1, keepdims=True)
    a = a / jnp.sqrt(diagonal)
    upper_ref[...] = jnp.where(lanes >= ranks, a, 0.0)

    @pl.when(mine < slots)
    def _():
        for i in range(n):
            total = a[i : i + 1, n : n + 1][None] * cols_ref[slot(0)]
            for j in range(1, i + 1):
                total = total + a[i : i + 1, n + j : n + j + 1][None] * cols_ref[slot(j)]
            result[i] = total

            @pl.when((me != i) | away)
            def _():
                remote(
                    result.at[i], window(out_ref, mine), s_back, r_back, {"vec": i, "space": block}
                ).start()

            @pl.when((me == i) & stay)
            def _():
                window(out_ref, mine)[...] = total

    def drain(several, fewer, sem):
        @pl.when(fewer)
        def _():
            await_bytes(result.at[pl.ds(0, several - 1)], sem)

        @pl.when(jnp.logical_not(fewer))
        def _():
            await_bytes(result.at[pl.ds(0, several)], sem)

    drain(slots, stay & (mine < slots), r_back)
    drain(slots, mine < slots, s_vec)

    @pl.when(mine < slots)
    def _():
        drain(n, stay, s_back)

    if packed:
        await_bytes(gvec.at[pl.ds(0, n * ns - 1)], s_gv)
    else:
        await_bytes(gspace.at[pl.ds(0, ns - 1)], s_gs)
        await_bytes(gvec.at[pl.ds(0, n - 1)], s_gv)


def body(n, ns, perturbation, trajectory, step_order):
    pert, traj = perturbation[0], trajectory[0]
    fields, rows, cols = pert.shape
    sections = traj.shape[0]
    chunks, bf = STEPS * sections * (fields // 2), traj.dtype
    packed = n * n <= 128 and n % 8 == 0 and n * ns <= 64
    size_f, size_l = slice_shape(n, fields, cols)
    vmem = pl.BlockSpec(memory_space=pltpu.VMEM)
    hbm = pl.BlockSpec(memory_space=pl.ANY)
    piece = pltpu.VMEM((chunks, rows, cols), bf)
    full = pltpu.VMEM((fields, rows + 2 * HALO, cols), F32)
    slices = pltpu.VMEM((n, size_f, rows, 128 * size_l), F32)
    small = pltpu.VMEM((n, 128), F32)
    dma, one = pltpu.SemaphoreType.DMA, pltpu.SemaphoreType.DMA(())
    out, upper = pl.pallas_call(
        functools.partial(whole_kernel, n, ns, float(fields * rows * cols * ns)),
        out_shape=(
            jax.ShapeDtypeStruct(pert.shape, F32),
            jax.ShapeDtypeStruct((n, 128), F32),
        ),
        in_specs=[pl.BlockSpec(memory_space=pltpu.SMEM), hbm, hbm],
        out_specs=(vmem, vmem),
        scratch_shapes=[
            pltpu.VMEM((STEPS * sections, fields, rows + 2 * HALO, cols), bf),
            pltpu.VMEM((2, sections * (fields // 2), rows, cols), bf),
            piece, piece, piece, piece, piece,
            pltpu.VMEM((fields // 2, rows + 4 * HALO, cols), bf),
            pltpu.VMEM((STEPS * sections, fields, 2 * HALO, cols), bf),
            full, full,
            pltpu.VMEM(pert.shape, F32), slices, slices,
            pltpu.VMEM((ns, n, 128), F32),
            pltpu.VMEM((n * ns, 1, 128) if packed else (n, n, 128), F32),
            small,
            pltpu.VMEM((1, 128), F32) if packed else small,
            dma((sections * (fields // 2),)), dma((chunks,)), dma((chunks,)), dma((STEPS * sections,)),
            one, one, one, one, one,
            one, one, one, one, one, one, one, one, one, one,
        ],
        compiler_params=pltpu.CompilerParams(collective_id=0, has_side_effects=True),
        name="whole",
    )(step_order, traj, pert)

    def finish(back_ref, upper_ref, out_ref, factor_ref):
        out_ref[...] = back_ref[...]
        factor_ref[...] = upper_ref[:, :n]

    out, factor = pl.pallas_call(
        finish,
        out_shape=(jax.ShapeDtypeStruct(pert.shape, F32), jax.ShapeDtypeStruct((n, n), F32)),
        in_specs=[vmem, vmem],
        out_specs=(vmem, vmem),
        name="finish",
    )(out, upper)
    return out[None], factor


def solution(mesh):
    n, ns = mesh.shape["vec"], mesh.shape["space"]
    in_specs = (P("vec", None, "space", None), P("vec", None, None, "space", None), P())
    out_specs = (P("vec", None, "space", None), P())
    return jax.shard_map(
        functools.partial(body, n, ns), mesh=mesh, in_specs=in_specs, out_specs=out_specs, check_vma=False
    )
```

time: 58.4 us -> 59.1 us (1.012)
  Pallas kernels: 57.6 us -> 58.3 us
    pallas_call x1, Pallas kernels: 55.9 us -> 56.6 us  [body(): pl.pallas_call(functools.partial(whole_kernel, n, ns, float(fields * rows...]
where the time goes in v1:
time: 59.1 us; the launch traced here: 58.9 us
  Pallas kernels  58.3 us (99%)
  between operations  0.64 us (1%)
    pallas_call x1, Pallas kernels, body(): pl.pallas_call(functools.partial(whole_kernel, n, ns, float(fields * rows...  56.6 us
    pallas_call x1, Pallas kernels, body(): pl.pallas_call(finish, out_shape=(jax.ShapeDtypeStruct(pert.shape, F32),...  1.7 us

profile of v1, /device:TPU:0, one launch (start us, length us, event | category | flops | bytes accessed | tf_op | source)
XLA Modules:
  0.0 58.9 jit_solution(344741629426108288)
XLA Ops:
  0.6 56.6 %whole.1 = (f32[6,24,512]{2,1,0:T(8,128)}, f32[8,128]{1,0:T(8,128)}) custom-call(s32[8]{0:T(128)} %order_ref.1, bf16[3,6,24,512]{3,2,1,0:T(8,128)(2,1)} %bitcast.3, f32[6,24,512]{2,1,0:T(8,128)} %bitcast.4), custom_call_target="tpu_custom_call" | custom-call | tf_op jit(solution)/shard_map/whole/pallas_call | solution.py:483
  57.2 1.7 %finish.1 = (f32[6,24,512]{2,1,0:T(8,128)}, f32[8,8]{1,0:T(8,128)}) custom-call(f32[6,24,512]{2,1,0:T(8,128)} %get-tuple-element.6.back_ref, f32[8,128]{1,0:T(8,128)} %get-tuple-element.7.upper_ref), custom_call_target="tpu_custom_call" | custom-call | tf_op jit(solution)/shard_map/finish/pallas_call | solution.py:515

commit v2 on v1

--- a/solution.py
+++ b/solution.py
@@ -9,8 +9,8 @@
 
 STEPS = 2
 SECTIONS = 3
-LAG = 4
-RUN_LAG = 3
+LAG = 6
+RUN_LAG = 7
 HALO = 8
 
 GRAVITY_TOP = 1.0
@@ -423,7 +423,7 @@
         a = a - factor * pivot_row
     diagonal = jnp.sum(jnp.where(lanes == ranks, a, 0.0), axis=1, keepdims=True)
     a = a / jnp.sqrt(diagonal)
-    upper_ref[...] = jnp.where(lanes >= ranks, a, 0.0)
+    upper_ref[...] = jnp.where(lanes >= ranks, a, 0.0)[:, :n]
 
     @pl.when(mine < slots)
     def _():
@@ -433,15 +433,18 @@
                 total = total + a[i : i + 1, n + j : n + j + 1][None] * cols_ref[slot(j)]
             result[i] = total
 
+        for d in range(n):
+            i = lax.rem(vector + n // 2 + d, n)
+
             @pl.when((me != i) | away)
             def _():
                 remote(
                     result.at[i], window(out_ref, mine), s_back, r_back, {"vec": i, "space": block}
                 ).start()
 
-            @pl.when((me == i) & stay)
-            def _():
-                window(out_ref, mine)[...] = total
+        @pl.when(stay)
+        def _():
+            window(out_ref, mine)[...] = result[me]
 
     def drain(several, fewer, sem):
         @pl.when(fewer)
@@ -482,10 +485,7 @@
     dma, one = pltpu.SemaphoreType.DMA, pltpu.SemaphoreType.DMA(())
     out, upper = pl.pallas_call(
         functools.partial(whole_kernel, n, ns, float(fields * rows * cols * ns)),
-        out_shape=(
-            jax.ShapeDtypeStruct(pert.shape, F32),
-            jax.ShapeDtypeStruct((n, 128), F32),
-        ),
+        out_shape=(pltpu.VMEM(pert.shape, F32), pltpu.VMEM((n, n), F32)),
         in_specs=[pl.BlockSpec(memory_space=pltpu.SMEM), hbm, hbm],
         out_specs=(vmem, vmem),
         scratch_shapes=[
@@ -508,17 +508,27 @@
         name="whole",
     )(step_order, traj, pert)
 
-    def finish(back_ref, upper_ref, out_ref, factor_ref):
-        out_ref[...] = back_ref[...]
-        factor_ref[...] = upper_ref[:, :n]
+    def finish(back_ref, upper_ref, out_ref, factor_ref, sems):
+        copies = [
+            pltpu.make_async_copy(back_ref, out_ref, sems.at[0]),
+            pltpu.make_async_copy(upper_ref, factor_ref, sems.at[1]),
+        ]
+        for copy in copies:
+            copy.start()
+        for copy in copies:
+            copy.wait()
 
     out, factor = pl.pallas_call(
         finish,
         out_shape=(jax.ShapeDtypeStruct(pert.shape, F32), jax.ShapeDtypeStruct((n, n), F32)),
         in_specs=[vmem, vmem],
-        out_specs=(vmem, vmem),
+        out_specs=(hbm, hbm),
+        scratch_shapes=[dma((2,))],
         name="finish",
-    )(out, upper)
+    )(
+        pltpu.with_memory_space_constraint(out, pltpu.VMEM),
+        pltpu.with_memory_space_constraint(upper, pltpu.VMEM),
+    )
     return out[None], factor
 
 

time: 59.1 us -> 54.8 us (0.927)
  Pallas kernels: 58.3 us -> 54 us
    pallas_call x1, Pallas kernels: 56.6 us -> 53.2 us  [body(): pl.pallas_call(functools.partial(whole_kernel, n, ns, float(fields * rows...]
    pallas_call x1, Pallas kernels: 1.7 us -> 0.74 us  [body(): pl.pallas_call(finish, out_shape=(jax.ShapeDtypeStruct(pert.shape, F32),...]
where the time goes in v2:
time: 54.8 us; the launch traced here: 54.6 us
  Pallas kernels  54 us (99%)
  between operations  0.64 us (1%)
    pallas_call x1, Pallas kernels, body(): pl.pallas_call(functools.partial(whole_kernel, n, ns, float(fields * rows...  53.2 us

profile of v2, /device:TPU:0, one launch (start us, length us, event | category | flops | bytes accessed | tf_op | source)
XLA Modules:
  0.0 54.6 jit_solution(1649204265163475625)
XLA Ops:
  0.6 53.2 %whole.1 = (f32[6,24,512]{2,1,0:T(8,128)S(1)}, f32[8,8]{1,0:T(8,128)S(1)}) custom-call(s32[8]{0:T(128)} %order_ref.1, bf16[3,6,24,512]{3,2,1,0:T(8,128)(2,1)} %bitcast.3, f32[6,24,512]{2,1,0:T(8,128)} %bitcast.4), custom_call_target="tpu_custom_call" | custom-call | tf_op jit(solution)/shard_map/whole/pallas_call | solution.py:486
  53.9 0.7 %finish.1 = (f32[6,24,512]{2,1,0:T(8,128)}, f32[8,8]{1,0:T(8,128)}) custom-call(f32[6,24,512]{2,1,0:T(8,128)S(1)} %get-tuple-element.6.back_ref, f32[8,8]{1,0:T(8,128)S(1)} %get-tuple-element.7.upper_ref), custom_call_target="tpu_custom_call" | custom-call | tf_op jit(solution)/shard_map/finish/pallas_call | solution.py:521

commit v3 on v2

--- a/solution.py
+++ b/solution.py
@@ -10,7 +10,8 @@
 STEPS = 2
 SECTIONS = 3
 LAG = 6
-RUN_LAG = 7
+RUN_LAG_END = 8
+RUN_LAG_MID = 15
 HALO = 8
 
 GRAVITY_TOP = 1.0
@@ -44,25 +45,20 @@
     return 0.5 * (pltpu.roll(field, count - 1, 1) - pltpu.roll(field, 1, 1))
 
 
-def tangent(base, state):
-    dp_top = GRAVITY_TOP * (state[0] + state[3])
-    dp_low = dp_top + GRAVITY_LOW * state[3]
-    rates = []
-    for layer, (mean_depth, pressure) in enumerate(((DEPTH_TOP, dp_top), (DEPTH_LOW, dp_low))):
-        at = 3 * layer
-        depth = base[at] + mean_depth
-        u, v = base[at + 1], base[at + 2]
-        dh, du, dv = state[at], state[at + 1], state[at + 2]
-        rates.append(-diff_x(depth * du + dh * u) - diff_y(depth * dv + dh * v))
-        rates.append(
-            -(u * diff_x(du) + du * diff_x(u)) - (v * diff_y(du) + dv * diff_y(u))
-            + CORIOLIS * dv - diff_x(pressure)
-        )
-        rates.append(
-            -(u * diff_x(dv) + du * diff_x(v)) - (v * diff_y(dv) + dv * diff_y(v))
-            - CORIOLIS * du - diff_y(pressure)
-        )
-    return rates
+def tangent(layer, base, state, top, low):
+    pressure = GRAVITY_TOP * (top + low)
+    if layer:
+        pressure = pressure + GRAVITY_LOW * low
+    depth = base[0] + (DEPTH_TOP, DEPTH_LOW)[layer]
+    u, v = base[1], base[2]
+    dh, du, dv = state
+    return [
+        -diff_x(depth * du + dh * u) - diff_y(depth * dv + dh * v),
+        -(u * diff_x(du) + du * diff_x(u)) - (v * diff_y(du) + dv * diff_y(u))
+        + CORIOLIS * dv - diff_x(pressure),
+        -(u * diff_x(dv) + du * diff_x(v)) - (v * diff_y(dv) + dv * diff_y(v))
+        - CORIOLIS * du - diff_y(pressure),
+    ]
 
 
 def slice_shape(n, fields, cols):
@@ -82,8 +78,8 @@
     out_ref, upper_ref,
     main, cand, in_up, in_dn, out_up, out_dn, pool, fresh, rims, anchor, work,
     x_ref, cols_ref, result, gspace, gvec, mine_s, mine_v,
-    r_cand, r_up, r_dn, r_sec, r_pert, r_vec, r_gs, r_gv, r_back,
-    s_cand, s_pert, s_up, s_dn, s_give, s_edge, s_vec, s_gs, s_gv, s_back,
+    r_cand, r_up, r_dn, r_sec, r_pert, r_side, r_vec, r_gs, r_gv, r_back,
+    s_cand, s_pert, s_side, s_up, s_dn, s_give, s_edge, s_vec, s_gs, s_gv, s_back,
 ):
     me = lax.axis_index("vec")
     tile = lax.axis_index("space")
@@ -122,7 +118,7 @@
     for across in range(2):
         for step in near:
             for c in range(2):
-                if across == 0 and step == 0 and c == 0:
+                if (across == 0 and step == 0 and c == 0) or (across and step):
                     continue
                 where = {
                     "vec": me + across * (1 - 2 * side),
@@ -174,17 +170,6 @@
                     {"vec": other, "space": 2 * place + c},
                 ).start()
 
-    next_tile = lax.rem(tile + 1, ns)
-    prev_tile = lax.rem(tile + ns - 1, ns)
-    remote(
-        pert_ref.at[:, pl.ds(rows - HALO, HALO)], anchor.at[:, pl.ds(0, HALO)], s_pert, r_pert,
-        worker(me, next_tile),
-    ).start()
-    remote(
-        pert_ref.at[:, pl.ds(0, HALO)], anchor.at[:, pl.ds(HALO + rows, HALO)], s_pert, r_pert,
-        worker(me, prev_tile),
-    ).start()
-
     @pl.when(away)
     def _():
         remote(
@@ -212,35 +197,43 @@
     last_block = worker(vector, lax.rem(block + ns - 1, ns))
     own_layer = pl.ds(half * core, half)
 
+    run_lag = jnp.where(up_ok & dn_ok, RUN_LAG_MID, RUN_LAG_END)
     near_lag = LAG * jnp.minimum(line, lines - 1 - line)
     far_lag = LAG * jnp.maximum(line, lines - 1 - line)
 
-    def advance(number, section, last):
-        base = [main[number, f].astype(F32) for f in range(fields)]
-        current = [work[f] for f in range(fields)]
-        change = tangent(base, current)
-        if last:
-            keep, take = 1.0 / 3.0, 2.0 / 3.0
-            mid = slice(HALO, HALO + rows)
-            for f in range(fields):
-                x_ref[f] = keep * anchor[f, mid] + take * (current[f][mid] + TIME_STEP * change[f][mid])
-            return
+    def rates(number, layer):
+        now = lax.rem(number, 2)
+        at = half * layer
+        base = [main[number, at + f].astype(F32) for f in range(half)]
+        state = [work[now, at + f] for f in range(half)]
+        top = state[0] if layer == 0 else work[now, 0]
+        low = state[0] if layer == 1 else work[now, half]
+        return state, tangent(layer, base, state, top, low)
+
+    def advance(number, layer):
+        section = lax.rem(number, SECTIONS)
+        state, change = rates(number, layer)
         keep = jnp.where(section == 0, 0.0, jnp.where(section == 1, 0.75, 1.0 / 3.0)).astype(F32)
         take = jnp.where(section == 0, 1.0, jnp.where(section == 1, 0.25, 2.0 / 3.0)).astype(F32)
-        for f in range(fields):
-            work[f] = keep * anchor[f] + take * (current[f] + TIME_STEP * change[f])
+        for f in range(half):
+            at = half * layer + f
+            work[1 - lax.rem(number, 2), at] = keep * anchor[at] + take * (state[f] + TIME_STEP * change[f])
 
         @pl.when(section == SECTIONS - 1)
         def _():
-            anchor[...] = work[...]
-
-    @pl.loop(0, LAG * (lines - 1) + chunks + RUN_LAG)
+            for f in range(half):
+                at = half * layer + f
+                anchor[at] = work[1 - lax.rem(number, 2), at]
+
+    most = max(LAG * (lines - 1) + RUN_LAG_END, LAG * max(lines - 2, 1) + RUN_LAG_MID)
+
+    @pl.loop(0, most + chunks - half + 1)
     def _(t):
         c_pair = t - near_lag
         c_up = t - LAG * line
         c_dn = t - LAG * (lines - 1 - line)
         c_fin = t - far_lag
-        c_run = c_fin - RUN_LAG
+        c_run = c_fin - run_lag
 
         @pl.when((c_pair >= 0) & (c_pair < parts))
         def _():
@@ -293,24 +286,29 @@
                             {"vec": target["vec"], "space": 2 * (target["space"] // 2) + c},
                         ).start()
 
+        @pl.when(c_fin == half - 1)
+        def _():
+            await_bytes(anchor.at[:, inner], r_pert)
+            for target, src, dst in ((first_block, rows, 0), (last_block, HALO, HALO + rows)):
+                remote(
+                    anchor.at[:, pl.ds(src, HALO)], anchor.at[:, pl.ds(dst, HALO)], s_side, r_side, target
+                ).start()
+
         @pl.when(c_run == half - 1)
         def _():
-            await_bytes(anchor, r_pert)
-            work[...] = anchor[...]
-
-        @pl.when(inside(c_run) & (lax.rem(c_run, half) == half - 1))
+            await_bytes(anchor.at[:, pl.ds(0, 2 * HALO)], r_side)
+            await_bytes(anchor.at[:, pl.ds(0, 2 * HALO)], s_side)
+            work[0] = anchor[...]
+
+        @pl.when((c_run >= half - 1) & (c_run < chunks - 1) & (lax.rem(c_run, half) == half - 1))
         def _():
             number = lax.div(c_run, half)
-            section = lax.rem(number, SECTIONS)
             await_bytes(fresh, r_sec.at[number])
-
-            @pl.when(c_run < chunks - 1)
-            def _():
-                advance(number, section, False)
-
-            @pl.when(c_run == chunks - 1)
-            def _():
-                advance(number, section, True)
+            advance(number, 0)
+
+        @pl.when((c_run >= half) & (c_run < chunks) & (lax.rem(c_run, half) == 0))
+        def _():
+            advance(lax.div(c_run, half) - 1, 1)
 
     size_f, size_l = slice_shape(n, fields, cols)
     across = cols // (128 * size_l)
@@ -330,13 +328,25 @@
         to = lax.rem(mine + d, n)
         return to, {"vec": 2 * (to // 2) + side, "space": 2 * place + lax.rem(to, 2)}
 
-    order = [d for d in sorted(range(1, n), key=lambda d: -min(d, n - d))]
-    for d in order:
-        to, where = spread(d)
-
-        @pl.when(to < slots)
-        def _():
-            remote(window(x_ref, to), cols_ref.at[slot(vector)], s_vec, r_vec, where).start()
+    order = [d for d in sorted(range(n), key=lambda d: -min(d, n - d))]
+    final = STEPS * SECTIONS - 1
+    await_bytes(fresh, r_sec.at[final])
+    mid = slice(HALO, HALO + rows)
+    for layer in range(2):
+        state, change = rates(final, layer)
+        for f in range(half):
+            at = half * layer + f
+            x_ref[at] = anchor[at, mid] * (1.0 / 3.0) + (2.0 / 3.0) * (state[f][mid] + TIME_STEP * change[f][mid])
+        if half % size_f and layer == 0:
+            continue
+        for d in order:
+            to, where = spread(d)
+            mine_now = (to < slots) & (to // across * size_f // half == layer) if half % size_f == 0 else to < slots
+            if d:
+
+                @pl.when(mine_now)
+                def _():
+                    remote(window(x_ref, to), cols_ref.at[slot(vector)], s_vec, r_vec, where).start()
 
     @pl.when(mine < slots)
     def _():
@@ -345,12 +355,11 @@
     @pl.when(stay)
     def _():
         await_bytes(pool.at[pl.ds(0, parts)], s_cand)
-        await_bytes(anchor.at[:, pl.ds(0, 2 * HALO)], s_pert)
 
     @pl.when(away)
     def _():
         await_bytes(pool.at[pl.ds(0, 2 * parts)], s_cand)
-        await_bytes(anchor, s_pert)
+        await_bytes(anchor.at[:, inner], s_pert)
 
     await_bytes(out_up, s_give)
     await_bytes(rims, s_edge)
@@ -416,12 +425,12 @@
             gram = gram + gvec[i]
 
     a = jnp.where(lanes < n, gram / entries, 0.0) + jnp.where(lanes == ranks + n, 1.0, 0.0)
+    diagonal = jnp.ones((n, 1), F32)
     for k in range(n):
-        pivot_row = a[k : k + 1, :]
-        column = jnp.sum(jnp.where(lanes == k, a, 0.0), axis=1, keepdims=True)
+        column = a[:, k : k + 1]
+        diagonal = jnp.where(ranks[:, :1] == k, column, diagonal)
         factor = jnp.where(ranks[:, :1] > k, column / column[k : k + 1, :], 0.0)
-        a = a - factor * pivot_row
-    diagonal = jnp.sum(jnp.where(lanes == ranks, a, 0.0), axis=1, keepdims=True)
+        a = a - factor * a[k : k + 1, :]
     a = a / jnp.sqrt(diagonal)
     upper_ref[...] = jnp.where(lanes >= ranks, a, 0.0)[:, :n]
 
@@ -494,15 +503,15 @@
             piece, piece, piece, piece, piece,
             pltpu.VMEM((fields // 2, rows + 4 * HALO, cols), bf),
             pltpu.VMEM((STEPS * sections, fields, 2 * HALO, cols), bf),
-            full, full,
+            full, pltpu.VMEM((2, *full.shape), F32),
             pltpu.VMEM(pert.shape, F32), slices, slices,
             pltpu.VMEM((ns, n, 128), F32),
             pltpu.VMEM((n * ns, 1, 128) if packed else (n, n, 128), F32),
             small,
             pltpu.VMEM((1, 128), F32) if packed else small,
             dma((sections * (fields // 2),)), dma((chunks,)), dma((chunks,)), dma((STEPS * sections,)),
-            one, one, one, one, one,
-            one, one, one, one, one, one, one, one, one, one,
+            one, one, one, one, one, one,
+            one, one, one, one, one, one, one, one, one, one, one,
         ],
         compiler_params=pltpu.CompilerParams(collective_id=0, has_side_effects=True),
         name="whole",

time: 54.8 us -> 51.5 us (0.940)
  Pallas kernels: 54 us -> 50.7 us
    pallas_call x1, Pallas kernels: 53.2 us -> 50 us  [body(): pl.pallas_call(functools.partial(whole_kernel, n, ns, float(fields * rows...]
where the time goes in v3:
time: 51.5 us; the launch traced here: 51.3 us
  Pallas kernels  50.7 us (98%)
  between operations  0.64 us (1%)
    pallas_call x1, Pallas kernels, body(): pl.pallas_call(functools.partial(whole_kernel, n, ns, float(fields * rows...  50 us

profile of v3, /device:TPU:0, one launch (start us, length us, event | category | flops | bytes accessed | tf_op | source)
XLA Modules:
  0.0 51.3 jit_solution(15890710181274274276)
XLA Ops:
  0.6 50.0 %whole.1 = (f32[6,24,512]{2,1,0:T(8,128)S(1)}, f32[8,8]{1,0:T(8,128)S(1)}) custom-call(s32[8]{0:T(128)} %order_ref.1, bf16[3,6,24,512]{3,2,1,0:T(8,128)(2,1)} %bitcast.3, f32[6,24,512]{2,1,0:T(8,128)} %bitcast.4), custom_call_target="tpu_custom_call" | custom-call | tf_op jit(solution)/shard_map/whole/pallas_call | solution.py:495
  50.6 0.7 %finish.1 = (f32[6,24,512]{2,1,0:T(8,128)}, f32[8,8]{1,0:T(8,128)}) custom-call(f32[6,24,512]{2,1,0:T(8,128)S(1)} %get-tuple-element.6.back_ref, f32[8,8]{1,0:T(8,128)S(1)} %get-tuple-element.7.upper_ref), custom_call_target="tpu_custom_call" | custom-call | tf_op jit(solution)/shard_map/finish/pallas_call | solution.py:530

commit v4 on v3

--- a/solution.py
+++ b/solution.py
@@ -35,14 +35,14 @@
     pltpu.make_async_copy(ref, ref, sem).wait()
 
 
-def diff_x(field):
+def twice_dx(field):
     count = field.shape[0]
-    return 0.5 * (pltpu.roll(field, count - 1, 0) - pltpu.roll(field, 1, 0))
-
-
-def diff_y(field):
+    return pltpu.roll(field, count - 1, 0) - pltpu.roll(field, 1, 0)
+
+
+def twice_dy(field):
     count = field.shape[1]
-    return 0.5 * (pltpu.roll(field, count - 1, 1) - pltpu.roll(field, 1, 1))
+    return pltpu.roll(field, count - 1, 1) - pltpu.roll(field, 1, 1)
 
 
 def tangent(layer, base, state, top, low):
@@ -53,11 +53,11 @@
     u, v = base[1], base[2]
     dh, du, dv = state
     return [
-        -diff_x(depth * du + dh * u) - diff_y(depth * dv + dh * v),
-        -(u * diff_x(du) + du * diff_x(u)) - (v * diff_y(du) + dv * diff_y(u))
-        + CORIOLIS * dv - diff_x(pressure),
-        -(u * diff_x(dv) + du * diff_x(v)) - (v * diff_y(dv) + dv * diff_y(v))
-        - CORIOLIS * du - diff_y(pressure),
+        twice_dx(depth * du + dh * u) + twice_dy(depth * dv + dh * v),
+        (u * twice_dx(du) + du * twice_dx(u)) + (v * twice_dy(du) + dv * twice_dy(u))
+        + twice_dx(pressure) - (2 * CORIOLIS) * dv,
+        (u * twice_dx(dv) + du * twice_dx(v)) + (v * twice_dy(dv) + dv * twice_dy(v))
+        + twice_dy(pressure) + (2 * CORIOLIS) * du,
     ]
 
 
@@ -71,6 +71,21 @@
             if best is None or f * l < best[0] * best[1]:
                 best = (f, l)
     return best
+
+
+def paired(value, mask, count):
+    if count & (count - 1):
+        return lax.rem(value + mask, count)
+    made, bit = 0, 1
+    while bit < count:
+        digit = lax.rem(lax.div(value, bit), 2)
+        made = made + bit * (1 - digit if mask & bit else digit)
+        bit *= 2
+    return made
+
+
+def far_first(count):
+    return sorted(range(count), key=lambda m: (-m.bit_length(), m))
 
 
 def whole_kernel(
@@ -217,7 +232,7 @@
         take = jnp.where(section == 0, 1.0, jnp.where(section == 1, 0.25, 2.0 / 3.0)).astype(F32)
         for f in range(half):
             at = half * layer + f
-            work[1 - lax.rem(number, 2), at] = keep * anchor[at] + take * (state[f] + TIME_STEP * change[f])
+            work[1 - lax.rem(number, 2), at] = keep * anchor[at] + take * (state[f] - (0.5 * TIME_STEP) * change[f])
 
         @pl.when(section == SECTIONS - 1)
         def _():
@@ -325,10 +340,10 @@
         return ref.at[pl.ds(f, size_f), :, pl.ds(l, 128 * size_l)]
 
     def spread(d):
-        to = lax.rem(mine + d, n)
+        to = paired(mine, d, n)
         return to, {"vec": 2 * (to // 2) + side, "space": 2 * place + lax.rem(to, 2)}
 
-    order = [d for d in sorted(range(n), key=lambda d: -min(d, n - d))]
+    order = [2 * m + c for m in far_first(lines) for c in range(2)]
     final = STEPS * SECTIONS - 1
     await_bytes(fresh, r_sec.at[final])
     mid = slice(HALO, HALO + rows)
@@ -336,7 +351,7 @@
         state, change = rates(final, layer)
         for f in range(half):
             at = half * layer + f
-            x_ref[at] = anchor[at, mid] * (1.0 / 3.0) + (2.0 / 3.0) * (state[f][mid] + TIME_STEP * change[f][mid])
+            x_ref[at] = anchor[at, mid] * (1.0 / 3.0) + (2.0 / 3.0) * (state[f][mid] - (0.5 * TIME_STEP) * change[f][mid])
         if half % size_f and layer == 0:
             continue
         for d in order:
@@ -394,10 +409,9 @@
         row = jnp.sum(pltpu.roll(mine_s[...], 0, 1, stride=n, stride_axis=0), axis=0, keepdims=True)
         mine_v[...] = row
         rank = me * ns + tile
-        reach = [(dv, ds) for dv in range(n) for ds in range(ns) if dv or ds]
-        reach.sort(key=lambda e: -min(e[0], n - e[0]))
+        reach = [(2 * m + c, ds) for m in far_first(lines) for c in range(2) for ds in range(ns) if m or c or ds]
         for dv, ds in reach:
-            where = {"vec": lax.rem(me + dv, n), "space": lax.rem(tile + ds, ns)}
+            where = {"vec": paired(me, dv, n), "space": paired(tile, ds, ns)}
             remote(mine_v, gvec.at[rank], s_gv, r_gv, where).start()
         gvec[rank] = row
         await_bytes(gvec.at[pl.ds(0, n * ns - 1)], r_gv)
@@ -442,8 +456,8 @@
                 total = total + a[i : i + 1, n + j : n + j + 1][None] * cols_ref[slot(j)]
             result[i] = total
 
-        for d in range(n):
-            i = lax.rem(vector + n // 2 + d, n)
+        for d in order:
+            i = paired(vector, d, n)
 
             @pl.when((me != i) | away)
             def _():

time: 51.5 us -> 50.9 us (0.988)
  Pallas kernels: 50.7 us -> 50 us
    pallas_call x1, Pallas kernels: 50 us -> 49.3 us  [body(): pl.pallas_call(functools.partial(whole_kernel, n, ns, float(fields * rows...]
where the time goes in v4:
time: 50.9 us; the launch traced here: 50.7 us
  Pallas kernels  50 us (98%)
  between operations  0.64 us (1%)
    pallas_call x1, Pallas kernels, body(): pl.pallas_call(functools.partial(whole_kernel, n, ns, float(fields * rows...  49.3 us

profile of v4, /device:TPU:0, one launch (start us, length us, event | category | flops | bytes accessed | tf_op | source)
XLA Modules:
  0.0 50.7 jit_solution(17727839730163437749)
XLA Ops:
  0.6 49.3 %whole.1 = (f32[6,24,512]{2,1,0:T(8,128)S(1)}, f32[8,8]{1,0:T(8,128)S(1)}) custom-call(s32[8]{0:T(128)} %order_ref.1, bf16[3,6,24,512]{3,2,1,0:T(8,128)(2,1)} %bitcast.3, f32[6,24,512]{2,1,0:T(8,128)} %bitcast.4), custom_call_target="tpu_custom_call" | custom-call | tf_op jit(solution)/shard_map/whole/pallas_call | solution.py:509
  49.9 0.7 %finish.1 = (f32[6,24,512]{2,1,0:T(8,128)}, f32[8,8]{1,0:T(8,128)}) custom-call(f32[6,24,512]{2,1,0:T(8,128)S(1)} %get-tuple-element.6.back_ref, f32[8,8]{1,0:T(8,128)S(1)} %get-tuple-element.7.upper_ref), custom_call_target="tpu_custom_call" | custom-call | tf_op jit(solution)/shard_map/finish/pallas_call | solution.py:544

commit v5 on v4

--- a/solution.py
+++ b/solution.py
@@ -9,7 +9,8 @@
 
 STEPS = 2
 SECTIONS = 3
-LAG = 6
+LAG_UP = 6
+LAG_DN = 6
 RUN_LAG_END = 8
 RUN_LAG_MID = 15
 HALO = 8
@@ -89,11 +90,11 @@
 
 
 def whole_kernel(
-    n, ns, entries, order_ref, traj_ref, pert_ref,
+    n, ns, entries, order_in, traj_ref, pert_ref,
     out_ref, upper_ref,
-    main, cand, in_up, in_dn, out_up, out_dn, pool, fresh, rims, anchor, work,
+    order_ref, main, cand, in_up, in_dn, out_up, out_dn, pool, fresh, rims, anchor, work,
     x_ref, cols_ref, result, gspace, gvec, mine_s, mine_v,
-    r_cand, r_up, r_dn, r_sec, r_pert, r_side, r_vec, r_gs, r_gv, r_back,
+    r_order, r_cand, r_up, r_dn, r_sec, r_pert, r_side, r_vec, r_gs, r_gv, r_back,
     s_cand, s_pert, s_side, s_up, s_dn, s_give, s_edge, s_vec, s_gs, s_gv, s_back,
 ):
     me = lax.axis_index("vec")
@@ -151,6 +152,8 @@
         pl.semaphore_signal(barrier, inc=1, device_id={"vec": me - 2}, device_id_type=MESH)
 
     inner = pl.ds(HALO, rows)
+    order_copy = pltpu.make_async_copy(order_in, order_ref, r_order)
+    order_copy.start()
 
     @pl.when(stay)
     def _():
@@ -213,8 +216,14 @@
     own_layer = pl.ds(half * core, half)
 
     run_lag = jnp.where(up_ok & dn_ok, RUN_LAG_MID, RUN_LAG_END)
-    near_lag = LAG * jnp.minimum(line, lines - 1 - line)
-    far_lag = LAG * jnp.maximum(line, lines - 1 - line)
+    up_lag = LAG_UP * line
+    dn_lag = LAG_DN * (lines - 1 - line)
+    near_lag = jnp.where(up_ok & dn_ok, jnp.minimum(up_lag, dn_lag), 0)
+    far_lag = jnp.maximum(up_lag, dn_lag)
+    most = max(
+        max(LAG_UP * l, LAG_DN * (lines - 1 - l)) + (RUN_LAG_MID if 0 < l < lines - 1 else RUN_LAG_END)
+        for l in range(lines)
+    )
 
     def rates(number, layer):
         now = lax.rem(number, 2)
@@ -240,13 +249,13 @@
                 at = half * layer + f
                 anchor[at] = work[1 - lax.rem(number, 2), at]
 
-    most = max(LAG * (lines - 1) + RUN_LAG_END, LAG * max(lines - 2, 1) + RUN_LAG_MID)
+    order_copy.wait()
 
     @pl.loop(0, most + chunks - half + 1)
     def _(t):
         c_pair = t - near_lag
-        c_up = t - LAG * line
-        c_dn = t - LAG * (lines - 1 - line)
+        c_up = t - up_lag
+        c_dn = t - dn_lag
         c_fin = t - far_lag
         c_run = c_fin - run_lag
 
@@ -509,9 +518,10 @@
     out, upper = pl.pallas_call(
         functools.partial(whole_kernel, n, ns, float(fields * rows * cols * ns)),
         out_shape=(pltpu.VMEM(pert.shape, F32), pltpu.VMEM((n, n), F32)),
-        in_specs=[pl.BlockSpec(memory_space=pltpu.SMEM), hbm, hbm],
+        in_specs=[hbm, hbm, hbm],
         out_specs=(vmem, vmem),
         scratch_shapes=[
+            pltpu.SMEM(step_order.shape, jnp.int32),
             pltpu.VMEM((STEPS * sections, fields, rows + 2 * HALO, cols), bf),
             pltpu.VMEM((2, sections * (fields // 2), rows, cols), bf),
             piece, piece, piece, piece, piece,
@@ -523,7 +533,7 @@
             pltpu.VMEM((n * ns, 1, 128) if packed else (n, n, 128), F32),
             small,
             pltpu.VMEM((1, 128), F32) if packed else small,
-            dma((sections * (fields // 2),)), dma((chunks,)), dma((chunks,)), dma((STEPS * sections,)),
+            one, dma((sections * (fields // 2),)), dma((chunks,)), dma((chunks,)), dma((STEPS * sections,)),
             one, one, one, one, one, one,
             one, one, one, one, one, one, one, one, one, one, one,
         ],

time: 50.9 us -> 50.3 us (0.988)
  Pallas kernels: 50 us -> 49.4 us
    pallas_call x1, Pallas kernels: 49.3 us -> 48.6 us  [body(): pl.pallas_call(functools.partial(whole_kernel, n, ns, float(fields * rows...]
where the time goes in v5:
time: 50.3 us; the launch traced here: 50 us
  Pallas kernels  49.4 us (98%)
  between operations  0.64 us (1%)
    pallas_call x1, Pallas kernels, body(): pl.pallas_call(functools.partial(whole_kernel, n, ns, float(fields * rows...  48.6 us

profile of v5, /device:TPU:0, one launch (start us, length us, event | category | flops | bytes accessed | tf_op | source)
XLA Modules:
  0.0 50.0 jit_solution(6283225809096836656)
XLA Ops:
  0.6 48.6 %whole.1 = (f32[6,24,512]{2,1,0:T(8,128)S(1)}, f32[8,8]{1,0:T(8,128)S(1)}) custom-call(s32[8]{0:T(128)} %order_in.1, bf16[3,6,24,512]{3,2,1,0:T(8,128)(2,1)} %bitcast.3, f32[6,24,512]{2,1,0:T(8,128)} %bitcast.4), custom_call_target="tpu_custom_call" | custom-call | tf_op jit(solution)/shard_map/whole/pallas_call | solution.py:518
  49.3 0.7 %finish.1 = (f32[6,24,512]{2,1,0:T(8,128)}, f32[8,8]{1,0:T(8,128)}) custom-call(f32[6,24,512]{2,1,0:T(8,128)S(1)} %get-tuple-element.6.back_ref, f32[8,8]{1,0:T(8,128)S(1)} %get-tuple-element.7.upper_ref), custom_call_target="tpu_custom_call" | custom-call | tf_op jit(solution)/shard_map/finish/pallas_call | solution.py:554

commit v6 on v5

--- a/solution.py
+++ b/solution.py
@@ -12,7 +12,7 @@
 LAG_UP = 6
 LAG_DN = 6
 RUN_LAG_END = 8
-RUN_LAG_MID = 15
+RUN_LAG_MID = 17
 HALO = 8
 
 GRAVITY_TOP = 1.0
@@ -101,8 +101,9 @@
     tile = lax.axis_index("space")
     fields, rows, cols = pert_ref.shape
     half = fields // 2
-    chunks = STEPS * SECTIONS * half
-    parts = SECTIONS * half
+    per = rows // HALO
+    parts = SECTIONS * per
+    chunks = STEPS * parts
     lines, places = n // 2, ns // 2
     side, line = lax.rem(me, 2), me // 2
     core, place = lax.rem(tile, 2), tile // 2
@@ -152,6 +153,13 @@
         pl.semaphore_signal(barrier, inc=1, device_id={"vec": me - 2}, device_id_type=MESH)
 
     inner = pl.ds(HALO, rows)
+
+    def band(w):
+        return pl.multiple_of(HALO * jnp.where(w == 0, 0, jnp.where(w == 1, per - 1, w - 1)), HALO)
+
+    def origin(p, layer):
+        return traj_ref.at[lax.div(p, per), pl.ds(half * layer, half), pl.ds(band(lax.rem(p, per)), HALO)]
+
     order_copy = pltpu.make_async_copy(order_in, order_ref, r_order)
     order_copy.start()
 
@@ -159,8 +167,7 @@
     def _():
         @pl.loop(0, parts)
         def _(p):
-            k, f = lax.div(p, half), lax.rem(p, half)
-            pltpu.make_async_copy(traj_ref.at[k, half * core + f], cand.at[0, p], r_cand.at[p]).start()
+            pltpu.make_async_copy(origin(p, core), cand.at[0, p], r_cand.at[p]).start()
 
         pltpu.make_async_copy(pert_ref, anchor.at[:, inner], r_pert).start()
 
@@ -172,19 +179,17 @@
     def _():
         @pl.loop(0, parts)
         def _(p):
-            k, f = lax.div(p, half), lax.rem(p, half)
             remote(
-                traj_ref.at[k, half * (1 - core) + f], cand.at[0, p], s_cand, r_cand.at[p], sibling
+                origin(p, 1 - core), cand.at[0, p], s_cand, r_cand.at[p], sibling
             ).start()
 
     @pl.when(away)
     def _():
         @pl.loop(0, parts)
         def _(p):
-            k, f = lax.div(p, half), lax.rem(p, half)
             for c in range(2):
                 remote(
-                    traj_ref.at[k, half * c + f], cand.at[1, p], s_cand, r_cand.at[p],
+                    origin(p, c), cand.at[1, p], s_cand, r_cand.at[p],
                     {"vec": other, "space": 2 * place + c},
                 ).start()
 
@@ -251,7 +256,7 @@
 
     order_copy.wait()
 
-    @pl.loop(0, most + chunks - half + 1)
+    @pl.loop(0, most + chunks - per + 1)
     def _(t):
         c_pair = t - near_lag
         c_up = t - up_lag
@@ -290,19 +295,18 @@
         @pl.when(inside(c_fin))
         def _():
             at = lax.div(owner_of(c_fin), 2)
-            q, f = lax.div(c_fin, half), half * core + lax.rem(c_fin, half)
-            main[q, f, inner] = jnp.where(
+            q, w = lax.div(c_fin, per), lax.rem(c_fin, per)
+            spot = main.at[q, own_layer, pl.ds(HALO + band(w), HALO)]
+            spot[...] = jnp.where(
                 at == line, candidate(c_fin), jnp.where(at < line, in_up[c_fin], in_dn[c_fin])
             )
-            spot = main.at[q, f, inner]
             remote(spot, spot, s_give, r_sec.at[q], sibling).start()
 
-            @pl.when(lax.rem(c_fin, half) == half - 1)
-            def _():
-                for c in range(2):
-                    for target, src, dst in (
-                        (first_block, rows, 0), (last_block, HALO, HALO + rows)
-                    ):
+            for turn, target, src, dst in ((0, last_block, HALO, HALO + rows), (1, first_block, rows, 0)):
+
+                @pl.when(w == turn)
+                def _():
+                    for c in range(2):
                         remote(
                             main.at[q, own_layer, pl.ds(src, HALO)],
                             main.at[q, own_layer, pl.ds(dst, HALO)],
@@ -310,7 +314,7 @@
                             {"vec": target["vec"], "space": 2 * (target["space"] // 2) + c},
                         ).start()
 
-        @pl.when(c_fin == half - 1)
+        @pl.when(c_fin == per - 1)
         def _():
             await_bytes(anchor.at[:, inner], r_pert)
             for target, src, dst in ((first_block, rows, 0), (last_block, HALO, HALO + rows)):
@@ -318,21 +322,21 @@
                     anchor.at[:, pl.ds(src, HALO)], anchor.at[:, pl.ds(dst, HALO)], s_side, r_side, target
                 ).start()
 
-        @pl.when(c_run == half - 1)
+        @pl.when(c_run == per - 1)
         def _():
             await_bytes(anchor.at[:, pl.ds(0, 2 * HALO)], r_side)
             await_bytes(anchor.at[:, pl.ds(0, 2 * HALO)], s_side)
             work[0] = anchor[...]
 
-        @pl.when((c_run >= half - 1) & (c_run < chunks - 1) & (lax.rem(c_run, half) == half - 1))
-        def _():
-            number = lax.div(c_run, half)
+        @pl.when((c_run >= per - 1) & (c_run < chunks - 1) & (lax.rem(c_run, per) == per - 1))
+        def _():
+            number = lax.div(c_run, per)
             await_bytes(fresh, r_sec.at[number])
             advance(number, 0)
 
-        @pl.when((c_run >= half) & (c_run < chunks) & (lax.rem(c_run, half) == 0))
-        def _():
-            advance(lax.div(c_run, half) - 1, 1)
+        @pl.when((c_run >= per) & (c_run < chunks) & (lax.rem(c_run, per) == 0))
+        def _():
+            advance(lax.div(c_run, per) - 1, 1)
 
     size_f, size_l = slice_shape(n, fields, cols)
     across = cols // (128 * size_l)
@@ -505,12 +509,13 @@
     pert, traj = perturbation[0], trajectory[0]
     fields, rows, cols = pert.shape
     sections = traj.shape[0]
-    chunks, bf = STEPS * sections * (fields // 2), traj.dtype
+    parts, bf = sections * (rows // HALO), traj.dtype
+    chunks, layer = STEPS * parts, fields // 2
     packed = n * n <= 128 and n % 8 == 0 and n * ns <= 64
     size_f, size_l = slice_shape(n, fields, cols)
     vmem = pl.BlockSpec(memory_space=pltpu.VMEM)
     hbm = pl.BlockSpec(memory_space=pl.ANY)
-    piece = pltpu.VMEM((chunks, rows, cols), bf)
+    piece = pltpu.VMEM((chunks, layer, HALO, cols), bf)
     full = pltpu.VMEM((fields, rows + 2 * HALO, cols), F32)
     slices = pltpu.VMEM((n, size_f, rows, 128 * size_l), F32)
     small = pltpu.VMEM((n, 128), F32)
@@ -523,7 +528,7 @@
         scratch_shapes=[
             pltpu.SMEM(step_order.shape, jnp.int32),
             pltpu.VMEM((STEPS * sections, fields, rows + 2 * HALO, cols), bf),
-            pltpu.VMEM((2, sections * (fields // 2), rows, cols), bf),
+            pltpu.VMEM((2, parts, layer, HALO, cols), bf),
             piece, piece, piece, piece, piece,
             pltpu.VMEM((fields // 2, rows + 4 * HALO, cols), bf),
             pltpu.VMEM((STEPS * sections, fields, 2 * HALO, cols), bf),
@@ -533,7 +538,7 @@
             pltpu.VMEM((n * ns, 1, 128) if packed else (n, n, 128), F32),
             small,
             pltpu.VMEM((1, 128), F32) if packed else small,
-            one, dma((sections * (fields // 2),)), dma((chunks,)), dma((chunks,)), dma((STEPS * sections,)),
+            one, dma((parts,)), dma((chunks,)), dma((chunks,)), dma((STEPS * sections,)),
             one, one, one, one, one, one,
             one, one, one, one, one, one, one, one, one, one, one,
         ],

time: 50.3 us -> 49.8 us (0.990)
  no operation moved by 1% of the time
where the time goes in v6:
time: 49.8 us; the launch traced here: 49.6 us
  Pallas kernels  49 us (98%)
  between operations  0.64 us (1%)
    pallas_call x1, Pallas kernels, body(): pl.pallas_call(functools.partial(whole_kernel, n, ns, float(fields * rows...  48.2 us

profile of v6, /device:TPU:0, one launch (start us, length us, event | category | flops | bytes accessed | tf_op | source)
XLA Modules:
  0.0 49.6 jit_solution(8141960714377025443)
XLA Ops:
  0.6 48.2 %whole.1 = (f32[6,24,512]{2,1,0:T(8,128)S(1)}, f32[8,8]{1,0:T(8,128)S(1)}) custom-call(s32[8]{0:T(128)} %order_in.1, bf16[3,6,24,512]{3,2,1,0:T(8,128)(2,1)} %bitcast.3, f32[6,24,512]{2,1,0:T(8,128)} %bitcast.4), custom_call_target="tpu_custom_call" | custom-call | tf_op jit(solution)/shard_map/whole/pallas_call | solution.py:523
  48.9 0.7 %finish.1 = (f32[6,24,512]{2,1,0:T(8,128)}, f32[8,8]{1,0:T(8,128)}) custom-call(f32[6,24,512]{2,1,0:T(8,128)S(1)} %get-tuple-element.6.back_ref, f32[8,8]{1,0:T(8,128)S(1)} %get-tuple-element.7.upper_ref), custom_call_target="tpu_custom_call" | custom-call | tf_op jit(solution)/shard_map/finish/pallas_call | solution.py:559

commit v7 on v6

--- a/solution.py
+++ b/solution.py
@@ -341,7 +341,11 @@
     size_f, size_l = slice_shape(n, fields, cols)
     across = cols // (128 * size_l)
     slots = (fields // size_f) * across
-    mine = 2 * line + core
+
+    def share(v):
+        return lines * lax.rem(v, 2) + lax.div(v, 2)
+
+    mine = share(2 * line + core)
     packed = n * n <= 128 and n % 8 == 0 and n * ns <= 64
 
     def slot(v):
@@ -353,8 +357,8 @@
         return ref.at[pl.ds(f, size_f), :, pl.ds(l, 128 * size_l)]
 
     def spread(d):
-        to = paired(mine, d, n)
-        return to, {"vec": 2 * (to // 2) + side, "space": 2 * place + lax.rem(to, 2)}
+        to = paired(2 * line + core, d, n)
+        return share(to), {"vec": 2 * (to // 2) + side, "space": 2 * place + lax.rem(to, 2)}
 
     order = [2 * m + c for m in far_first(lines) for c in range(2)]
     final = STEPS * SECTIONS - 1

time: 49.8 us -> 49.5 us (level)
  no operation moved by 1% of the time
where the time goes in v7:
time: 49.5 us; the launch traced here: 49.4 us
  Pallas kernels  48.7 us (98%)
  between operations  0.64 us (1%)
    pallas_call x1, Pallas kernels, body(): pl.pallas_call(functools.partial(whole_kernel, n, ns, float(fields * rows...  48 us

profile of v7, /device:TPU:0, one launch (start us, length us, event | category | flops | bytes accessed | tf_op | source)
XLA Modules:
  0.0 49.4 jit_solution(17144990674302583383)
XLA Ops:
  0.6 48.0 %whole.1 = (f32[6,24,512]{2,1,0:T(8,128)S(1)}, f32[8,8]{1,0:T(8,128)S(1)}) custom-call(s32[8]{0:T(128)} %order_in.1, bf16[3,6,24,512]{3,2,1,0:T(8,128)(2,1)} %bitcast.3, f32[6,24,512]{2,1,0:T(8,128)} %bitcast.4), custom_call_target="tpu_custom_call" | custom-call | tf_op jit(solution)/shard_map/whole/pallas_call | solution.py:527
  48.6 0.7 %finish.1 = (f32[6,24,512]{2,1,0:T(8,128)}, f32[8,8]{1,0:T(8,128)}) custom-call(f32[6,24,512]{2,1,0:T(8,128)S(1)} %get-tuple-element.6.back_ref, f32[8,8]{1,0:T(8,128)S(1)} %get-tuple-element.7.upper_ref), custom_call_target="tpu_custom_call" | custom-call | tf_op jit(solution)/shard_map/finish/pallas_call | solution.py:563

commit v8 on v7

--- a/solution.py
+++ b/solution.py
@@ -432,9 +432,11 @@
             remote(mine_v, gvec.at[rank], s_gv, r_gv, where).start()
         gvec[rank] = row
         await_bytes(gvec.at[pl.ds(0, n * ns - 1)], r_gv)
-        row = gvec[0]
-        for i in range(1, n * ns):
-            row = row + gvec[i]
+        rows_in = [gvec[i] for i in range(n * ns)]
+        while len(rows_in) > 1:
+            pairs = [a + b for a, b in zip(rows_in[::2], rows_in[1::2])]
+            rows_in = pairs + rows_in[len(pairs) * 2 :]
+        row = rows_in[0]
         gram = pltpu.roll(jnp.broadcast_to(row, (n, 128)), 128 - n * (n - 1), 1, stride=n, stride_axis=0)
     else:
         for d in range(1, ns):

time: 49.5 us -> 49.5 us (level)
  no operation moved by 1% of the time
where the time goes in v8:
time: 49.5 us; the launch traced here: 49.3 us
  Pallas kernels  48.7 us (98%)
  between operations  0.64 us (1%)
    pallas_call x1, Pallas kernels, body(): pl.pallas_call(functools.partial(whole_kernel, n, ns, float(fields * rows...  48 us

profile of v8, /device:TPU:0, one launch (start us, length us, event | category | flops | bytes accessed | tf_op | source)
XLA Modules:
  0.0 49.3 jit_solution(13163197510837383570)
XLA Ops:
  0.6 48.0 %whole.1 = (f32[6,24,512]{2,1,0:T(8,128)S(1)}, f32[8,8]{1,0:T(8,128)S(1)}) custom-call(s32[8]{0:T(128)} %order_in.1, bf16[3,6,24,512]{3,2,1,0:T(8,128)(2,1)} %bitcast.3, f32[6,24,512]{2,1,0:T(8,128)} %bitcast.4), custom_call_target="tpu_custom_call" | custom-call | tf_op jit(solution)/shard_map/whole/pallas_call | solution.py:529
  48.6 0.7 %finish.1 = (f32[6,24,512]{2,1,0:T(8,128)}, f32[8,8]{1,0:T(8,128)}) custom-call(f32[6,24,512]{2,1,0:T(8,128)S(1)} %get-tuple-element.6.back_ref, f32[8,8]{1,0:T(8,128)S(1)} %get-tuple-element.7.upper_ref), custom_call_target="tpu_custom_call" | custom-call | tf_op jit(solution)/shard_map/finish/pallas_call | solution.py:565
